TPU v7x, 128 devices: a whole 4x4x4 slice. The times are simulated.
128 devices in a mesh: fsdp: 2 (over y_hi), tile: 32 (over z, x, core), scan: 2 (over y_lo).
Axes of the slice: x: 4, y: 4 (y_hi: 2, y_lo: 2; y = y_hi * 2 + y_lo), z: 4, core: 2. Of those that a mesh axis runs over, the one named last changes fastest.
Arguments:
- acts: bfloat16 [2, 2, 16, 64, 64, 512], P('scan', 'fsdp', None, 'tile'), may hold values from -6 to 6
- spatial_weight: bfloat16 [9, 512, 512], P(None, None, 'fsdp'), may hold values from -0.09375 to 0.09375
- temporal_weight: bfloat16 [3, 512, 512], P(None, None, 'fsdp'), may hold values from -0.15625 to 0.15625
- readout_weight: bfloat16 [2, 4096, 512], P('scan', 'tile'), may hold values from -0.25 to 0.25
- readout_bias: bfloat16 [2, 4096], P('scan', 'tile'), may hold values from -1.5 to 0.5
- tile_of: int32 [2, 4096, 1], P('scan', 'tile'), may hold values from 0 to 31; in each aligned block of 128 rows (0 to 127, 128 to 255, ..., all dimensions but the last counted through in order) at most 10 rows name the same one
- row_of: int32 [2, 4096], P('scan', 'tile'), may hold values from 0 to 1
- column_of: int32 [2, 4096], P('scan', 'tile'), may hold values from 0 to 63
- spikes: int32 [2, 2, 16, 4096], P('scan', 'fsdp', None, 'tile'), may hold values from 0 to 5
Outputs:
- spatial_grad: float32 [9, 512, 512], P(None, None, 'fsdp')
- temporal_grad: float32 [3, 512, 512], P(None, None, 'fsdp')
- readout_grad: float32 [2, 4096, 512], P('scan', 'tile')
- bias_grad: float32 [2, 4096], P('scan', 'tile')
Inputs may be any that keep to these rules, and one draw needn't show every extreme that they name: `tile_of`: among the 128 neurons of one index of tile (aligned blocks of a scan's neurons), at most 10 read one tile.
All inputs are finite; a program needn't handle non-finite values.
Results may differ from a plain program's by a relative error of at most 0.006.
Values may be sent and summed in bfloat16 or wider, within the bound.
No kernel may reach another device: no remote copies, remote signals or barrier semaphores. Data moves between devices by JAX's collectives and lax.ppermute only.
A program may use at most 192 MiB of HBM per device.

v0:
```python
import jax
import jax.numpy as jnp
from jax import lax
from jax.sharding import PartitionSpec as P


def padded_2(block, sides, width):
    for axis, dim in sides:
        count = lax.axis_size(axis)
        forward = [(i, i + 1) for i in range(count - 1)]
        backward = [(target, source) for source, target in forward]
        low = lax.ppermute(
            lax.slice_in_dim(block, block.shape[dim] - width, None, axis=dim), axis, forward
        )
        high = lax.ppermute(lax.slice_in_dim(block, 0, width, axis=dim), axis, backward)
        block = jnp.concatenate([low, block, high], axis=dim)
    return block


def contract_rows(left, right):
    return lax.dot_general(
        left, right, (((0,), (0,)), ((), ())), preferred_element_type=jnp.float32
    )


def on_device(
    acts,
    spatial_weight,
    temporal_weight,
    readout_weight,
    readout_bias,
    tile_of,
    row_of,
    column_of,
    spikes,
):
    spatial, temporal = (
        lax.all_gather(spatial_weight, "fsdp", axis=2, tiled=True),
        lax.all_gather(temporal_weight, "fsdp", axis=2, tiled=True),
    )
    frames_in = acts[0, 0]
    frames, rows, width, channels = frames_in.shape
    cells = rows * width
    extended = padded_2(frames_in, (("tile", 1),), 1)
    padded = jnp.pad(extended, ((0, 0), (0, 0), (1, 1), (0, 0)))

    def patch(tap):
        return padded[:, tap // 3 : tap // 3 + rows, tap % 3 : tap % 3 + width, :].reshape(
            -1, channels
        )

    spatial_sum = jnp.zeros((frames * cells, channels), jnp.float32)
    for tap in range(9):
        spatial_sum = spatial_sum + jnp.dot(
            patch(tap), spatial[tap], preferred_element_type=jnp.float32
        )
    spatial_out = spatial_sum.astype(jnp.bfloat16).reshape(frames, cells, channels)
    causal = jnp.pad(spatial_out, ((2, 0), (0, 0), (0, 0)))
    mixed = jnp.zeros((frames * cells, channels), jnp.float32)
    for lag in range(3):
        mixed = mixed + jnp.dot(
            causal[2 - lag : 2 - lag + frames].reshape(-1, channels),
            temporal[lag],
            preferred_element_type=jnp.float32,
        )
    mixed = mixed.reshape(frames, cells, channels)
    features = jax.nn.elu(mixed).astype(jnp.bfloat16)
    tile_count = lax.axis_size("tile")
    rep_count = lax.axis_size("fsdp")
    neurons = readout_weight.shape[1]
    capacity = max(2, 5 * neurons // (2 * tile_count))
    slot_count = tile_count * capacity
    scale_factor = 1.0 / (rep_count * frames)
    tile_ids = tile_of[0, :, 0]
    cell_ids = row_of[0] * width + column_of[0]
    onehot_tile = (tile_ids[:, None] == jnp.arange(tile_count)[None, :]).astype(jnp.int32)
    earlier = jnp.cumsum(onehot_tile, axis=0) - onehot_tile
    rank_ids = jnp.sum(earlier * onehot_tile, axis=1)
    slot_ids = tile_ids * capacity + rank_ids
    selector = slot_ids[None, :] == jnp.arange(slot_count)[:, None]
    weights_now = readout_weight[0]
    bias_now = readout_bias[0].astype(jnp.float32)
    counts_now = spikes[0, 0]
    wanted = jnp.sum(jnp.where(selector, cell_ids[None, :], 0), axis=1).reshape(
        tile_count, capacity
    )
    held_cells = lax.all_to_all(wanted, "tile", split_axis=0, concat_axis=0, tiled=True).reshape(-1)
    outgoing = features[:, held_cells, :].reshape(frames, tile_count, capacity, channels)
    arrived = lax.all_to_all(outgoing, "tile", split_axis=1, concat_axis=1, tiled=True).reshape(
        frames, slot_count, channels
    )
    picked = arrived[:, slot_ids, :]
    logits = (
        jnp.einsum("fnc,nc->fn", picked, weights_now, preferred_element_type=jnp.float32)
        + bias_now[None, :]
    )
    delta = (jnp.exp(logits) - counts_now.astype(jnp.float32)) * scale_factor
    weight_grad = jnp.einsum("fn,fnc->nc", delta, picked.astype(jnp.float32))
    bias_grad = jnp.sum(delta, axis=0)
    terms = (delta[:, :, None] * weights_now[None, :, :].astype(jnp.float32)).astype(jnp.bfloat16)
    placed = jnp.einsum(
        "sn,fnc->fsc", selector.astype(jnp.bfloat16), terms, preferred_element_type=jnp.float32
    ).astype(jnp.bfloat16)
    returned = lax.all_to_all(
        placed.reshape(frames, tile_count, capacity, channels),
        "tile",
        split_axis=1,
        concat_axis=1,
        tiled=True,
    )
    returned = returned.reshape(frames, slot_count, channels)
    scatter_table = (jnp.arange(cells)[:, None] == held_cells[None, :]).astype(jnp.bfloat16)
    feature_grad = jnp.einsum(
        "ks,fsc->fkc", scatter_table, returned, preferred_element_type=jnp.float32
    )
    weight_grad, bias_grad = lax.psum((weight_grad, bias_grad), "fsdp")
    slope = jnp.where(mixed > 0, 1.0, jnp.exp(jnp.minimum(mixed, 0.0)))
    mixed_grad = (feature_grad * slope).astype(jnp.bfloat16)
    flat_grad = mixed_grad.reshape(-1, channels)
    temporal_grad = jnp.stack(
        [
            contract_rows(causal[2 - lag : 2 - lag + frames].reshape(-1, channels), flat_grad)
            for lag in range(3)
        ]
    )
    back_pad = jnp.pad(mixed_grad, ((0, 2), (0, 0), (0, 0)))
    spatial_back = jnp.zeros((frames * cells, channels), jnp.float32)
    for lag in range(3):
        spatial_back = spatial_back + lax.dot_general(
            back_pad[lag : lag + frames].reshape(-1, channels),
            temporal[lag],
            (((1,), (1,)), ((), ())),
            preferred_element_type=jnp.float32,
        )
    spatial_back = spatial_back.astype(jnp.bfloat16)
    spatial_grad = jnp.stack([contract_rows(patch(tap), spatial_back) for tap in range(9)])
    shard_spatial, shard_temporal = (
        lax.psum_scatter(spatial_grad, "fsdp", scatter_dimension=2, tiled=True),
        lax.psum_scatter(temporal_grad, "fsdp", scatter_dimension=2, tiled=True),
    )
    total_spatial, total_temporal = lax.psum((shard_spatial, shard_temporal), ("tile", "scan"))
    return (total_spatial, total_temporal, weight_grad[None], bias_grad[None])


def solution(mesh):
    return jax.shard_map(
        on_device,
        mesh=mesh,
        in_specs=(
            P("scan", "fsdp", None, "tile", None, None),
            P(None, None, "fsdp"),
            P(None, None, "fsdp"),
            P("scan", "tile", None),
            P("scan", "tile"),
            P("scan", "tile", None),
            P("scan", "tile"),
            P("scan", "tile"),
            P("scan", "fsdp", None, "tile"),
        ),
        out_specs=(
            P(None, None, "fsdp"),
            P(None, None, "fsdp"),
            P("scan", "tile", None),
            P("scan", "tile"),
        ),
        check_vma=False,
    )
```

profile of v0, /device:TPU:1, one launch (start us, length us, event | category | flops | bytes accessed | tf_op | source)
XLA Modules:
  0.0 1104.2 jit_solution(8402206730829438454)
XLA Ops:
  7.9 0.8 copy-done
  8.8 1.5 fusion.57
  10.3 4.5 collective-permute-start
  14.8 1.9 collective-permute-start.1
  17.4 0.7 all_to_all.12
  18.1 8.6 all-to-all-start
  27.4 7.7 all-to-all-done
  36.5 3.5 fusion.7
  40.0 6.6 fusion.56
  46.7 3.6 pad_maximum_fusion.2
  50.2 29.1 %all-gather.3.cloned.1.call-done = bf16[9,512,512]{2,1,0:T(8,128)(2,1)} async-done(((bf16[9,512,256]{2,1,0:T(8,128)(2,1)}), bf16[9,512,512]{2,1,0:T(8,128)(2,1)}) %all-gather.3.cloned.1.call-update) | async-done | bytes 4718608 | tf_op jit(solution)/shard_map/all_gather | solution.py:38
  79.3 3.1 fusion.31
  83.1 1.3 fusion.32
  84.7 3.3 fusion.34
  88.1 3.2 fusion.35
  91.3 3.3 fusion.37
  94.5 3.3 fusion.30
  97.8 3.3 fusion.36
  101.1 3.3 fusion.33
  104.4 10.9 add_convert_fusion.1
  115.3 4.4 copy.22
  119.7 4.6 pad_slice_fusion.2
  124.2 3.9 copy.23
  128.1 3.9 copy.24
  132.1 3.1 fusion.39
  135.2 1.3 fusion.41
  136.8 1.3 add_add_fusion
  138.0 1.6 fusion.9
  140.0 2.5 copy.26
  142.6 5.2 gather_fusion
  147.8 8.4 all-to-all-start.1
  156.3 61.6 %all-to-all-done.1 = bf16[16,32,10,512]{3,0,2,1:T(8,128)(2,1)} async-done(((bf16[16,32,10,512]{3,0,2,1:T(8,128)(2,1)}), bf16[16,32,10,512]{3,0,2,1:T(8,128)(2,1)}, u32[]{:S(2)}, u32[]{:S(2)}) %all-to-all-start.1) | async-done | bytes 5242912 | tf_op jit(solution)/shard_map/all_to_all | solution.py:89
  217.9 4.5 gather_fusion.1
  222.4 2.3 fusion.14
  224.8 1.7 convert_bitcast_fusion
  226.5 5.3 copy.27
  231.8 8.7 all-to-all-start.2
  240.6 61.8 %all-to-all-done.2 = bf16[16,32,10,512]{3,0,2,1:T(8,128)(2,1)} async-done(((bf16[16,32,10,512]{3,0,2,1:T(8,128)(2,1)}), bf16[16,32,10,512]{3,0,2,1:T(8,128)(2,1)}, u32[]{:S(2)}, u32[]{:S(2)}) %all-to-all-start.2) | async-done | bytes 5242912 | tf_op jit(solution)/shard_map/all_to_all | solution.py:104
  302.4 8.1 fusion.11
  310.5 1.2 convolution_bitcast_fusion
  311.8 1.3 convolution_bitcast_fusion.1
  313.1 1.3 convolution_bitcast_fusion.2
  314.4 2.0 pad_maximum_fusion
  316.6 2.7 pad_slice_fusion
  319.8 1.3 fusion.38
  321.1 1.3 fusion.40
  322.4 1.3 add_convert_fusion
  324.1 2.2 fusion.28
  326.4 2.2 fusion.27
  328.6 2.3 fusion.26
  330.9 2.2 fusion.25
  333.1 2.3 fusion.24
  335.5 2.3 fusion.23
  337.7 2.2 fusion.22
  340.0 2.3 fusion.21
  342.3 2.3 fusion.20
  344.8 1.5 copy-done.21
  347.5 14.7 %reduce-scatter.5.cloned.1.call-done = f32[3,512,256]{2,1,0:T(8,128)} async-done(((f32[3,512,512]{2,1,0:T(8,128)}), f32[3,512,256]{2,1,0:T(8,128)}) %reduce-scatter.5.cloned.1.call-update) | async-done | bytes 1572880 | tf_op jit(solution)/shard_map/reduce_scatter | solution.py:139
  362.2 116.4 %reduce-scatter.3.cloned.1.call-done = f32[9,512,256]{2,1,0:T(8,128)} async-done(((f32[9,512,512]{2,1,0:T(8,128)}), f32[9,512,256]{2,1,0:T(8,128)}) %reduce-scatter.3.cloned.1.call-update) | async-done | bytes 4718608 | tf_op jit(solution)/shard_map/reduce_scatter | solution.py:138
  478.6 5.8 psum.31
  484.4 27.5 %all-reduce.7.cloned.1.call-done = f32[1,128,512]{2,1,0:T(8,128)} async-done(((f32[1,128,512]{2,1,0:T(8,128)}), f32[1,128,512]{2,1,0:T(8,128)}) %all-reduce.7.cloned.1.call-update) | async-done | bytes 262160 | tf_op jit(solution)/shard_map/psum | solution.py:116
  511.9 578.2 %all-reduce.9.cloned.1.call-done = (f32[9,512,256]{2,1,0:T(8,128)}, f32[3,512,256]{2,1,0:T(8,128)}) async-done(((f32[9,512,256]{2,1,0:T(8,128)}, f32[3,512,256]{2,1,0:T(8,128)}), (f32[9,512,256]{2,1,0:T(8,128)}, f32[3,512,256]{2,1,0:T(8,128)})) %all-reduce.9.cloned.1.call-update) | async-done | bytes 6291472 | tf_op jit(solution)/shard_map/psum | solution.py:141
  1090.1 4.9 copy.54
  1095.1 1.1 copy.55
  (103 shorter events, 8.7 us)
Async XLA Ops:
  7.2 1.6 copy-start
  7.2 72.2 %all-gather.3.cloned.1.call-start = ((), (), s32[]{:S(2)}) async-start(), calls=%async_computation.5 | async-start | bytes 7077888 | tf_op jit(solution)/shard_map/all_gather | solution.py:38
  8.8 8.0 copy-start.30
  8.8 8.4 copy-start.31
  8.8 8.4 copy-start.32
  10.3 26.2 %collective-permute-start = (bf16[16,1,64,512]{3,2,1,0:T(8,128)(2,1)}, bf16[16,1,64,512]{3,2,1,0:T(8,128)(2,1)S(1)}, u32[]{:S(2)}, u32[]{:S(2)}) collective-permute-start(bf16[16,1,64,512]{3,2,1,0:T(8,128)(2,1)} %get-tuple-element.20), channel_id=1, source_target_pairs={{0,2},{2,4},{4,6},{6,8},{8,10},{10,12},{12,14},{14,16},{16,18},{18... | collective-permute-start | bytes 3145736 | tf_op jit(solution)/shard_map/ppermute | solution.py:12
  14.8 21.7 %collective-permute-start.1 = (bf16[16,1,64,512]{3,2,1,0:T(8,128)(2,1)}, bf16[16,1,64,512]{3,2,1,0:T(8,128)(2,1)}, u32[]{:S(2)}, u32[]{:S(2)}) collective-permute-start(bf16[16,1,64,512]{3,2,1,0:T(8,128)(2,1)} %get-tuple-element.21), channel_id=1, source_target_pairs={{2,0},{4,2},{6,4},{8,6},{10,8},{12,10},{14,12},{16,14},{18,16},{20... | collective-permute-start | bytes 3145736 | tf_op jit(solution)/shard_map/ppermute | solution.py:15
  18.1 17.0 %all-to-all-start = ((s32[32,1,10]{2,1,0:T(1,128)}), s32[32,1,10]{2,1,0:T(1,128)S(1)}, u32[]{:S(2)}, u32[]{:S(2)}) async-start(s32[32,1,10]{2,1,0:T(1,128)} %bitcast.28), calls=%async_computation | async-start | bytes 32768 | tf_op jit(solution)/shard_map/all_to_all | solution.py:87
  26.7 105.4 %all-gather.5.cloned.1.call-start = ((), (), s32[]{:S(2)}) async-start(), calls=%async_computation.6 | async-start | bytes 2359296 | tf_op jit(solution)/shard_map/all_gather | solution.py:39
  79.3 3.1 copy-start.6
  79.3 3.8 copy-start.25
  83.1 1.6 copy-start.8
  84.7 3.3 copy-start.10
  88.0 3.2 copy-start.12
  91.3 3.3 copy-start.15
  94.5 3.3 copy-start.17
  101.1 3.3 copy-start.19
  132.1 3.1 copy-start.14
  132.1 3.1 copy-start.23
  135.2 1.6 copy-start.22
  138.0 2.0 copy-start.2
  147.8 8.4 copy-start.33
  147.8 8.4 copy-start.28
  147.8 70.1 %all-to-all-start.1 = ((bf16[16,32,10,512]{3,0,2,1:T(8,128)(2,1)}), bf16[16,32,10,512]{3,0,2,1:T(8,128)(2,1)}, u32[]{:S(2)}, u32[]{:S(2)}) async-start(bf16[16,32,10,512]{3,0,2,1:T(8,128)(2,1)} %bitcast.218), calls=%async_computation.1 | async-start | bytes 10485760 | tf_op jit(solution)/shard_map/all_to_all | solution.py:89
  222.4 2.4 copy-start.29
  231.8 70.6 %all-to-all-start.2 = ((bf16[16,32,10,512]{3,0,2,1:T(8,128)(2,1)}), bf16[16,32,10,512]{3,0,2,1:T(8,128)(2,1)}, u32[]{:S(2)}, u32[]{:S(2)}) async-start(bf16[16,32,10,512]{3,0,2,1:T(8,128)(2,1)} %bitcast.219), calls=%async_computation.2 | async-start | bytes 10485760 | tf_op jit(solution)/shard_map/all_to_all | solution.py:104
  240.5 121.7 %reduce-scatter.5.cloned.1.call-start = ((), (), s32[]{:S(2)}) async-start(), calls=%async_computation.8 | async-start | bytes 4718592 | tf_op jit(solution)/shard_map/reduce_scatter | solution.py:139
  302.4 8.1 copy-start.1
  310.5 2.5 copy-start.3
  316.4 162.3 %reduce-scatter.3.cloned.1.call-start = ((), (), s32[]{:S(2)}) async-start(), calls=%async_computation.7 | async-start | bytes 14155776 | tf_op jit(solution)/shard_map/reduce_scatter | solution.py:138
  316.6 2.7 copy-start.4
  316.6 3.2 copy-start.24
  322.4 1.7 copy-start.13
  324.1 2.3 copy-start.18
  326.4 2.2 copy-start.11
  328.6 2.3 copy-start.9
  333.1 2.3 copy-start.7
  335.5 2.3 copy-start.5
  337.7 2.2 copy-start.16
  340.0 2.3 copy-start.20
  344.6 1.7 copy-start.21
  344.6 167.3 %all-reduce.7.cloned.1.call-start = ((), (), s32[]{:S(2)}) async-start(), calls=%async_computation.9 | async-start | bytes 524288 | tf_op jit(solution)/shard_map/psum | solution.py:116
  347.5 742.7 %all-reduce.9.cloned.1.call-start = ((), (), s32[]{:S(2)}) async-start(), calls=%async_computation.10 | async-start | bytes 12582912 | tf_op jit(solution)/shard_map/psum | solution.py:141
  1090.1 4.9 copy-start.26
  1095.1 1.1 copy-start.27
Sparse Core Ops, SparseCore 0:
  9.6 69.6 all-gather.2
  81.0 30.5 all-gather.4
  316.5 45.6 reduce-scatter.4
  364.5 114.0 reduce-scatter.2
  481.5 30.4 all-reduce.6
  514.3 575.7 all-reduce.8
where the time goes:
time: 1110 us; the launch traced here: 1100 us
  waiting for transfers between devices  899 us (81%)
  matrix products  81.2 us (7%)
  local copies, waits for them, and re-layouts  59.2 us (5%)
  starting transfers between devices  32.5 us (3%)
  between operations  14.9 us (1%)
  other arithmetic  12 us (1%)
    psum x1, waiting for transfers between devices, on_device(): lax.psum((shard_spatial, shard_temporal), ('tile', 'scan'))  578 us
    reduce_scatter x1, waiting for transfers between devices, on_device(): lax.psum_scatter(spatial_grad, 'fsdp', scatter_dimension=2, tiled=True)  116 us
    all_to_all x1, waiting for transfers between devices, on_device(): lax.all_to_all(placed.reshape(frames, tile_count, capacity, channels), 't...  61.8 us
    all_to_all x1, waiting for transfers between devices, on_device(): lax.all_to_all(outgoing, 'tile', split_axis=1, concat_axis=1, tiled=True)  61.6 us
    dot_general x9, matrix products, on_device(): jnp.dot(patch(tap), spatial[tap], preferred_element_type=jnp.float32)  34.9 us
    all_gather x1, waiting for transfers between devices, on_device(): lax.all_gather(spatial_weight, 'fsdp', axis=2, tiled=True)  29.1 us
    psum x1, waiting for transfers between devices, on_device(): weight_grad, bias_grad = lax.psum((weight_grad, bias_grad), 'fsdp')  27.5 us
    dot_general x12, matrix products, contract_rows(): lax.dot_general(left, right, (((0,), (0,)), ((), ())), preferred_element_...  24.2 us
  transfers between devices with their start and end apart: 11, of which 8 were waited for; matrix products, arithmetic and copies ran while one was open for 9% of the time, Pallas kernels for 0%

commit v1 on v0

--- a/solution.py
+++ b/solution.py
@@ -101,12 +101,20 @@
     placed = jnp.einsum(
         "sn,fnc->fsc", selector.astype(jnp.bfloat16), terms, preferred_element_type=jnp.float32
     ).astype(jnp.bfloat16)
-    returned = lax.all_to_all(
-        placed.reshape(frames, tile_count, capacity, channels),
-        "tile",
-        split_axis=1,
-        concat_axis=1,
-        tiled=True,
+    returned = jnp.concatenate(
+        lax.all_to_all(
+            jnp.stack(
+                jnp.split(
+                    placed.reshape(frames, tile_count, capacity, channels),
+                    lax.axis_size("tile"),
+                    axis=1,
+                )
+            ),
+            "tile",
+            0,
+            0,
+        ),
+        axis=1,
     )
     returned = returned.reshape(frames, slot_count, channels)
     scatter_table = (jnp.arange(cells)[:, None] == held_cells[None, :]).astype(jnp.bfloat16)

time: 1110 us -> 1140 us (1.027)
  local copies, waits for them, and re-layouts: 59.2 us -> 80.8 us
    unnamed x71 -> x102, local copies, waits for them, and re-layouts: 11.8 us -> 33.5 us
where the time goes in v1:
time: 1140 us; the launch traced here: 1130 us
  waiting for transfers between devices  898 us (79%)
  matrix products  81.2 us (7%)
  local copies, waits for them, and re-layouts  80.8 us (7%)
  starting transfers between devices  32.7 us (3%)
  between operations  15 us (1%)
  other arithmetic  12 us (1%)
    psum x1, waiting for transfers between devices, on_device(): lax.psum((shard_spatial, shard_temporal), ('tile', 'scan'))  578 us
    reduce_scatter x1, waiting for transfers between devices, on_device(): lax.psum_scatter(spatial_grad, 'fsdp', scatter_dimension=2, tiled=True)  116 us
    all_to_all x1, waiting for transfers between devices, on_device(): lax.all_to_all(outgoing, 'tile', split_axis=1, concat_axis=1, tiled=True)  61.6 us
    all_to_all x1, waiting for transfers between devices, on_device(): lax.all_to_all(jnp.stack(jnp.split(placed.reshape(frames, tile_count, cap...  61.5 us
    dot_general x9, matrix products, on_device(): jnp.dot(patch(tap), spatial[tap], preferred_element_type=jnp.float32)  34.9 us
    unnamed x102, local copies, waits for them, and re-layouts  33.5 us
    all_gather x1, waiting for transfers between devices, on_device(): lax.all_gather(spatial_weight, 'fsdp', axis=2, tiled=True)  28.4 us
    psum x1, waiting for transfers between devices, on_device(): weight_grad, bias_grad = lax.psum((weight_grad, bias_grad), 'fsdp')  27.5 us
  transfers between devices with their start and end apart: 11, of which 8 were waited for; matrix products, arithmetic and copies ran while one was open for 9% of the time, Pallas kernels for 0%

profile of v1, /device:TPU:1, one launch (start us, length us, event | category | flops | bytes accessed | tf_op | source)
XLA Modules:
  0.0 1125.1 jit_solution(4054040922854783619)
XLA Ops:
  7.9 3.1 fusion.89
  11.0 4.5 collective-permute-start
  15.5 1.9 collective-permute-start.1
  18.1 0.7 all_to_all.12
  18.8 8.6 all-to-all-start
  28.1 7.7 all-to-all-done
  37.2 3.5 fusion.7
  40.8 6.6 fusion.88
  47.4 3.6 pad_maximum_fusion.2
  50.9 28.4 %all-gather.3.cloned.1.call-done = bf16[9,512,512]{2,1,0:T(8,128)(2,1)} async-done(((bf16[9,512,256]{2,1,0:T(8,128)(2,1)}), bf16[9,512,512]{2,1,0:T(8,128)(2,1)}) %all-gather.3.cloned.1.call-update) | async-done | bytes 4718608 | tf_op jit(solution)/shard_map/all_gather | solution.py:38
  79.4 3.1 fusion.31
  83.1 1.3 fusion.32
  84.7 3.3 fusion.34
  88.1 3.2 fusion.35
  91.3 3.3 fusion.37
  94.6 3.3 fusion.30
  97.9 3.3 fusion.36
  101.2 3.3 fusion.33
  104.4 10.9 add_convert_fusion.1
  115.4 4.4 copy.54
  119.7 4.6 pad_slice_fusion.2
  124.3 3.9 copy.55
  128.2 3.9 copy.56
  132.1 3.1 fusion.39
  135.2 1.3 fusion.41
  136.8 1.3 add_add_fusion
  138.1 2.0 copy-done.2
  140.1 1.6 fusion.9
  141.7 2.5 copy.58
  144.2 5.2 gather_fusion
  149.4 8.4 all-to-all-start.1
  157.9 61.6 %all-to-all-done.1 = bf16[16,32,10,512]{3,0,2,1:T(8,128)(2,1)} async-done(((bf16[16,32,10,512]{3,0,2,1:T(8,128)(2,1)}), bf16[16,32,10,512]{3,0,2,1:T(8,128)(2,1)}, u32[]{:S(2)}, u32[]{:S(2)}) %all-to-all-start.1) | async-done | bytes 5242912 | tf_op jit(solution)/shard_map/all_to_all | solution.py:89
  219.5 4.5 gather_fusion.1
  224.0 2.3 fusion.14
  226.4 1.7 convert_bitcast_fusion
  228.1 2.9 copy.59
  252.7 8.7 all-to-all-start.2
  261.7 61.5 %all-to-all-done.2 = bf16[32,16,1,10,512]{4,1,3,2,0:T(8,128)(2,1)} async-done(((bf16[32,16,1,10,512]{4,1,3,2,0:T(8,128)(2,1)}), bf16[32,16,1,10,512]{4,1,3,2,0:T(8,128)(2,1)}, u32[]{:S(2)}, u32[]{:S(2)}) %all-to-all-start.2) | async-done | bytes 5242912 | tf_op jit(solution)/shard_map/all_to_all | solution.py:105
  323.3 8.1 fusion.11
  331.4 1.2 convolution_bitcast_fusion
  332.6 1.3 convolution_bitcast_fusion.1
  333.9 1.3 convolution_bitcast_fusion.2
  335.2 2.0 pad_maximum_fusion
  337.5 2.7 pad_slice_fusion
  340.7 1.3 fusion.38
  342.0 1.3 fusion.40
  343.3 1.3 add_convert_fusion
  345.0 2.3 fusion.28
  347.3 2.2 fusion.27
  349.5 2.3 fusion.26
  351.8 2.2 fusion.25
  354.0 2.3 fusion.24
  356.4 2.3 fusion.23
  358.7 2.2 fusion.22
  360.9 2.3 fusion.21
  363.2 2.3 fusion.20
  365.7 1.5 copy-done.21
  368.4 14.7 %reduce-scatter.5.cloned.1.call-done = f32[3,512,256]{2,1,0:T(8,128)} async-done(((f32[3,512,512]{2,1,0:T(8,128)}), f32[3,512,256]{2,1,0:T(8,128)}) %reduce-scatter.5.cloned.1.call-update) | async-done | bytes 1572880 | tf_op jit(solution)/shard_map/reduce_scatter | solution.py:147
  383.1 116.4 %reduce-scatter.3.cloned.1.call-done = f32[9,512,256]{2,1,0:T(8,128)} async-done(((f32[9,512,512]{2,1,0:T(8,128)}), f32[9,512,256]{2,1,0:T(8,128)}) %reduce-scatter.3.cloned.1.call-update) | async-done | bytes 4718608 | tf_op jit(solution)/shard_map/reduce_scatter | solution.py:146
  499.5 5.8 psum.31
  505.3 27.5 %all-reduce.7.cloned.1.call-done = f32[1,128,512]{2,1,0:T(8,128)} async-done(((f32[1,128,512]{2,1,0:T(8,128)}), f32[1,128,512]{2,1,0:T(8,128)}) %all-reduce.7.cloned.1.call-update) | async-done | bytes 262160 | tf_op jit(solution)/shard_map/psum | solution.py:124
  532.8 578.2 %all-reduce.9.cloned.1.call-done = (f32[9,512,256]{2,1,0:T(8,128)}, f32[3,512,256]{2,1,0:T(8,128)}) async-done(((f32[9,512,256]{2,1,0:T(8,128)}, f32[3,512,256]{2,1,0:T(8,128)}), (f32[9,512,256]{2,1,0:T(8,128)}, f32[3,512,256]{2,1,0:T(8,128)})) %all-reduce.9.cloned.1.call-update) | async-done | bytes 6291472 | tf_op jit(solution)/shard_map/psum | solution.py:149
  1111.0 5.0 copy.117
  1116.0 1.1 copy.118
  (135 shorter events, 30.2 us)
Async XLA Ops:
  7.2 30.1 %copy-start = (bf16[1,1,16,2,64,512]{5,4,3,2,1,0:T(8,128)(2,1)S(1)}, bf16[1,1,16,2,64,512]{5,4,3,2,1,0:T(8,128)(2,1)}, u32[]{:S(2)}) copy-start(bf16[1,1,16,2,64,512]{5,4,3,2,1,0:T(8,128)(2,1)} %param.9) | copy-start | bytes 6291460
  7.2 10.3 copy-start.30
  7.2 10.7 copy-start.32
  7.2 10.7 copy-start.31
  7.2 72.2 %all-gather.3.cloned.1.call-start = ((), (), s32[]{:S(2)}) async-start(), calls=%async_computation.5 | async-start | bytes 7077888 | tf_op jit(solution)/shard_map/all_gather | solution.py:38
  11.0 26.2 %collective-permute-start = (bf16[16,1,64,512]{3,2,1,0:T(8,128)(2,1)}, bf16[16,1,64,512]{3,2,1,0:T(8,128)(2,1)S(1)}, u32[]{:S(2)}, u32[]{:S(2)}) collective-permute-start(bf16[16,1,64,512]{3,2,1,0:T(8,128)(2,1)} %get-tuple-element.20), channel_id=1, source_target_pairs={{0,2},{2,4},{4,6},{6,8},{8,10},{10,12},{12,14},{14,16},{16,18},{18... | collective-permute-start | bytes 3145736 | tf_op jit(solution)/shard_map/ppermute | solution.py:12
  15.5 21.7 %collective-permute-start.1 = (bf16[16,1,64,512]{3,2,1,0:T(8,128)(2,1)}, bf16[16,1,64,512]{3,2,1,0:T(8,128)(2,1)}, u32[]{:S(2)}, u32[]{:S(2)}) collective-permute-start(bf16[16,1,64,512]{3,2,1,0:T(8,128)(2,1)} %get-tuple-element.21), channel_id=1, source_target_pairs={{2,0},{4,2},{6,4},{8,6},{10,8},{12,10},{14,12},{16,14},{18,16},{20... | collective-permute-start | bytes 3145736 | tf_op jit(solution)/shard_map/ppermute | solution.py:15
  18.8 17.0 %all-to-all-start = ((s32[32,1,10]{2,1,0:T(1,128)}), s32[32,1,10]{2,1,0:T(1,128)S(1)}, u32[]{:S(2)}, u32[]{:S(2)}) async-start(s32[32,1,10]{2,1,0:T(1,128)} %bitcast.28), calls=%async_computation | async-start | bytes 32768 | tf_op jit(solution)/shard_map/all_to_all | solution.py:87
  27.4 104.7 %all-gather.5.cloned.1.call-start = ((), (), s32[]{:S(2)}) async-start(), calls=%async_computation.6 | async-start | bytes 2359296 | tf_op jit(solution)/shard_map/all_gather | solution.py:39
  79.4 3.1 copy-start.6
  79.4 3.8 copy-start.25
  83.1 1.6 copy-start.8
  84.7 3.4 copy-start.10
  88.1 3.2 copy-start.12
  91.3 3.3 copy-start.15
  94.6 3.3 copy-start.17
  101.2 3.3 copy-start.19
  132.1 3.1 copy-start.14
  132.1 3.1 copy-start.23
  135.2 1.6 copy-start.22
  138.1 2.0 copy-start.2
  149.4 8.4 copy-start.33
  149.4 8.4 copy-start.28
  149.4 70.1 %all-to-all-start.1 = ((bf16[16,32,10,512]{3,0,2,1:T(8,128)(2,1)}), bf16[16,32,10,512]{3,0,2,1:T(8,128)(2,1)}, u32[]{:S(2)}, u32[]{:S(2)}) async-start(bf16[16,32,10,512]{3,0,2,1:T(8,128)(2,1)} %bitcast.380), calls=%async_computation.1 | async-start | bytes 10485760 | tf_op jit(solution)/shard_map/all_to_all | solution.py:89
  157.8 68.6 %copy-start.29 = (s32[1,1,16,128]{3,2,1,0:T(8,128)S(1)}, s32[1,1,16,128]{3,2,1,0:T(8,128)}, u32[]{:S(2)}) copy-start(s32[1,1,16,128]{3,2,1,0:T(8,128)} %param.17) | copy-start | bytes 24580
  252.7 70.6 %all-to-all-start.2 = ((bf16[32,16,1,10,512]{4,1,3,2,0:T(8,128)(2,1)}), bf16[32,16,1,10,512]{4,1,3,2,0:T(8,128)(2,1)}, u32[]{:S(2)}, u32[]{:S(2)}) async-start(bf16[32,16,1,10,512]{4,1,3,2,0:T(8,128)(2,1)} %fusion.43), calls=%async_computation.2 | async-start | bytes 10485760 | tf_op jit(solution)/shard_map/all_to_all | solution.py:105
  261.3 121.7 %reduce-scatter.5.cloned.1.call-start = ((), (), s32[]{:S(2)}) async-start(), calls=%async_computation.8 | async-start | bytes 4718592 | tf_op jit(solution)/shard_map/reduce_scatter | solution.py:147
  323.3 8.1 copy-start.1
  331.4 2.5 copy-start.3
  337.2 162.3 %reduce-scatter.3.cloned.1.call-start = ((), (), s32[]{:S(2)}) async-start(), calls=%async_computation.7 | async-start | bytes 14155776 | tf_op jit(solution)/shard_map/reduce_scatter | solution.py:146
  337.5 2.7 copy-start.4
  337.5 3.2 copy-start.24
  343.3 1.8 copy-start.13
  345.0 2.3 copy-start.18
  347.3 2.2 copy-start.11
  349.5 2.3 copy-start.9
  354.0 2.3 copy-start.7
  356.4 2.3 copy-start.5
  358.6 2.2 copy-start.16
  360.9 2.3 copy-start.20
  365.5 1.7 copy-start.21
  365.6 167.2 %all-reduce.7.cloned.1.call-start = ((), (), s32[]{:S(2)}) async-start(), calls=%async_computation.9 | async-start | bytes 524288 | tf_op jit(solution)/shard_map/psum | solution.py:124
  368.4 742.6 %all-reduce.9.cloned.1.call-start = ((), (), s32[]{:S(2)}) async-start(), calls=%async_computation.10 | async-start | bytes 12582912 | tf_op jit(solution)/shard_map/psum | solution.py:149
  1111.0 5.0 copy-start.26
  1111.0 6.1 copy-start.27
Sparse Core Ops, SparseCore 0:
  9.7 69.6 all-gather.2
  81.0 30.5 all-gather.4
  337.3 45.7 reduce-scatter.4
  385.4 114.0 reduce-scatter.2
  502.3 30.4 all-reduce.6
  535.2 575.7 all-reduce.8
